TPU v7x, 32 devices: a whole 2x2x4 slice. The times are simulated.
32 devices in a mesh: groups: 2 (over y), expert: 4 (over z), token: 4 (over x, core).
Axes of the slice: x: 2, y: 2, z: 4, core: 2. Of those that a mesh axis runs over, the one named last changes fastest.
Arguments:
- tokens: bfloat16 [512, 2048], P(('groups', 'expert'), 'token'), parts along dimension 0, may hold values from -6 to 6
- expert_ids: int32 [512, 8], P(('groups', 'expert')), parts along dimension 0, may hold values from 0 to 15, all different within a row; in each aligned block of 64 rows (0 to 63, 64 to 127, ...) at most 64 rows name the same one
- route_weights: float32 [512, 8], P(('groups', 'expert')), parts along dimension 0, may hold values from 0.1 to 0.4
- w_gate_up: bfloat16 [16, 2048, 1536], P('expert', 'token'), may hold values from -0.125 to 0.125
- w_down: bfloat16 [16, 768, 2048], P('expert', None, 'token'), may hold values from -0.21875 to 0.21875
Outputs:
- combined: bfloat16 [512, 2048], P(('groups', 'expert'), 'token'), parts along dimension 0
There are 2 independent parts, one for each index of `groups`. A program takes and returns all parts, laid end to end along the dimension named above; an argument that names none is the same for every part. Nothing has to cross between parts.
Inputs may be any that keep to these rules, and one draw needn't show every extreme that they name: `expert_ids`: each row names 8 different experts. In each aligned block of 64 rows no expert is named by more than 64 rows, a bound that some block reaches.
All inputs are finite; a program needn't handle non-finite values.
Results may differ from a plain program's by a relative error of at most 0.02.
Values may be sent and summed in bfloat16 or wider, within the bound.
A program may use at most 64 MiB of HBM per device.

v0:
```python
import jax
import jax.numpy as jnp
from jax import lax
from jax.sharding import PartitionSpec as P


def rank_slots(flat_ids, experts):
    onehot = (flat_ids[:, None] == jnp.arange(experts, dtype=jnp.int32)[None, :]).astype(jnp.int32)
    rank_of = jnp.sum((jnp.cumsum(onehot, axis=0) - 1) * onehot, axis=1)
    return (onehot, rank_of)


def gate_up_terms(inputs, w_gate_up):
    return jnp.einsum("erd,edf->ref", inputs, w_gate_up, preferred_element_type=jnp.float32)


def expert_block(inputs, gate_up_w, down_w):
    hidden_units = gate_up_w.shape[2] // 2
    summed = lax.psum_scatter(
        gate_up_terms(inputs, gate_up_w).astype(jnp.bfloat16),
        "token",
        scatter_dimension=0,
        tiled=True,
    ).astype(jnp.float32)
    hidden = (jax.nn.silu(summed[..., :hidden_units]) * summed[..., hidden_units:]).astype(
        jnp.bfloat16
    )
    produced = jnp.einsum(
        "reh,ehd->erd",
        lax.all_gather(hidden, "token", axis=0, tiled=True),
        down_w,
        preferred_element_type=jnp.float32,
    )
    return produced.astype(jnp.bfloat16)


def per_device(tokens, expert_ids, route_weights, w_gate_up, w_down):
    tok_dev, feature_cols = tokens.shape
    top_k = expert_ids.shape[1]
    local_experts = w_gate_up.shape[0]
    n_expert = lax.axis_size("expert")
    experts = local_experts * n_expert
    capacity = max(2, min(tok_dev, tok_dev * top_k * 5 // (2 * experts)))
    slot_count = n_expert * capacity
    flat_ids = expert_ids.reshape(-1)
    onehot, rank_of = rank_slots(flat_ids, experts)
    position = (
        flat_ids % local_experts * slot_count + flat_ids // local_experts * capacity + rank_of
    )
    token_of = jnp.arange(flat_ids.shape[0], dtype=jnp.int32) // top_k
    slot_table = (
        jnp.full((local_experts * slot_count,), tok_dev, jnp.int32).at[position].set(token_of)
    )
    padded = jnp.concatenate([tokens, jnp.zeros((1, feature_cols), tokens.dtype)], axis=0)
    outgoing = jnp.take(padded, slot_table, axis=0).reshape(
        local_experts, n_expert, capacity, feature_cols
    )
    arrived = lax.all_to_all(outgoing, "expert", split_axis=1, concat_axis=1, tiled=True)
    inputs = arrived.reshape(local_experts, slot_count, feature_cols)
    expert_out = expert_block(inputs, w_gate_up, w_down)
    returned = lax.all_to_all(
        expert_out.reshape(local_experts, n_expert, capacity, feature_cols),
        "expert",
        split_axis=1,
        concat_axis=1,
        tiled=True,
    )
    picked = jnp.take(
        returned.reshape(local_experts * slot_count, feature_cols), position, axis=0
    ).reshape(tok_dev, top_k, feature_cols)
    combined = jnp.sum(route_weights[:, :, None] * picked.astype(jnp.float32), axis=1)
    return combined.astype(jnp.bfloat16)


def solution(mesh):
    return jax.shard_map(
        per_device,
        mesh=mesh,
        in_specs=(
            P(("groups", "expert"), "token"),
            P(("groups", "expert"), None),
            P(("groups", "expert"), None),
            P("expert", "token", None),
            P("expert", None, "token"),
        ),
        out_specs=P(("groups", "expert"), "token"),
        check_vma=False,
    )
```

profile of v0, /device:TPU:0, one launch (start us, length us, event | category | flops | bytes accessed | tf_op | source)
XLA Modules:
  0.0 166.3 jit_solution(5265012218865901291)
XLA Ops:
  6.5 0.9 copy.31
  7.5 0.1 eq.28
  7.6 0.1 reshape.180
  7.6 0.1 reshape.182
  7.8 1.2 reduce-window.6
  8.9 0.2 slice_reduce_fusion
  9.2 0.1 fusion.7
  9.3 2.4 %scatter_custom_fusion = s32[1024]{0:T(1024)S(1)} fusion(s32[512]{0:T(512)S(1)} %bitcast.36, s32[512]{0:T(512)S(1)} %add_select_fusion.2, s32[]{:T(128)} %constant.82.clone.1), kind=kCustom, calls=%fused_computation.54 | custom fusion | bytes 4100 | tf_op jit(solution)/shard_map/scatter | solution.py:52
  11.9 0.8 concatenate.3
  12.7 5.1 %gather_fusion = bf16[1024,512]{1,0:T(8,128)(2,1)} fusion(bf16[65,512]{1,0:T(8,128)(2,1)S(1)} %concatenate.3, s32[1024]{0:T(1024)S(1)} %fusion.13), kind=kCustom, calls=%fused_computation | custom fusion | bytes 2101248 | tf_op jit(solution)/shard_map/jit(_take)/gather | solution.py:55
  17.8 1.4 copy_select_fusion
  19.2 31.9 %all_to_all.10 = bf16[4,4,64,512]{3,2,0,1:T(8,128)(2,1)S(1)} all-to-all(bf16[4,4,64,512]{3,2,0,1:T(8,128)(2,1)S(1)} %copy_select_fusion), channel_id=1, replica_groups=mesh['groups'=2,'expert'=4,'token'=4] {'expert'}, dimensions={1} | all-to-all | bytes 2097152 | tf_op jit(solution)/shard_map/all_to_all | solution.py:58
  51.2 6.3 %fusion = bf16[256,4,1536]{2,0,1:T(8,128)(2,1)} fusion(bf16[4,256,512]{2,1,0:T(8,128)(2,1)S(1)} %bitcast.33, bf16[4,512,1536]{2,1,0:T(8,128)(2,1)} %param.8), kind=kOutput, calls=%fused_computation.4 | convolution fusion | flops 1612185600 | bytes 10485760 | tf_op jit(solution)/shard_map/erd,edf->ref/dot_general | solution.py:14
  57.5 37.0 %reduce-scatter.2.cloned.1.call-done = bf16[64,4,1536]{2,0,1:T(8,128)(2,1)} async-done(((bf16[256,4,1536]{2,0,1:T(8,128)(2,1)}), bf16[64,4,1536]{2,0,1:T(8,128)(2,1)}) %reduce-scatter.2.cloned.1.call-update) | async-done | bytes 786448 | tf_op jit(solution)/shard_map/reduce_scatter | solution.py:19
  94.5 1.3 convert_element_type.29
  95.8 1.0 fusion.1
  96.8 19.8 %all-gather.2.cloned.1.call-done = bf16[256,4,768]{2,0,1:T(8,128)(2,1)} async-done(((bf16[64,4,768]{2,0,1:T(8,128)(2,1)}), bf16[256,4,768]{2,0,1:T(8,128)(2,1)}) %all-gather.2.cloned.1.call-update) | async-done | bytes 1572880 | tf_op jit(solution)/shard_map/all_gather | solution.py:30
  116.6 2.4 %convolution_convert_fusion.1 = bf16[4,256,512]{2,1,0:T(8,128)(2,1)S(1)} fusion(bf16[256,4,768]{2,0,1:T(8,128)(2,1)} %all-gather.2.cloned.1.call-done, bf16[4,768,512]{2,1,0:T(8,128)(2,1)S(1)} %copy-done), kind=kOutput, calls=%fused_computation.5 | convolution fusion | flops 805830656 | bytes 5767168 | tf_op jit(solution)/shard_map/reh,ehd->erd/dot_general | solution.py:28
  119.0 1.1 copy.42
  120.1 4.6 %all-to-all-start.1 = ((bf16[4,4,64,512]{3,2,0,1:T(8,128)(2,1)}), bf16[4,4,64,512]{3,2,0,1:T(8,128)(2,1)}, u32[]{:S(2)}, u32[]{:S(2)}) async-start(bf16[4,4,64,512]{3,2,0,1:T(8,128)(2,1)} %copy.42), calls=%async_computation.2 | async-start | bytes 2097152 | tf_op jit(solution)/shard_map/all_to_all | solution.py:61
  125.0 26.0 %all-to-all-done.1 = bf16[4,4,64,512]{3,2,0,1:T(8,128)(2,1)} async-done(((bf16[4,4,64,512]{3,2,0,1:T(8,128)(2,1)}), bf16[4,4,64,512]{3,2,0,1:T(8,128)(2,1)}, u32[]{:S(2)}, u32[]{:S(2)}) %all-to-all-start.1) | async-done | bytes 1048608 | tf_op jit(solution)/shard_map/all_to_all | solution.py:61
  151.0 2.4 %copy.43 = bf16[4,4,64,512]{3,2,1,0:T(8,128)(2,1)} copy(bf16[4,4,64,512]{3,2,0,1:T(8,128)(2,1)} %all-to-all-done.1) | data formatting | bytes 2097152 | tf_op jit(solution)/shard_map/all_to_all | solution.py:61
  153.3 4.0 %gather_fusion.1 = bf16[512,512]{1,0:T(8,128)(2,1)} fusion(bf16[1024,512]{1,0:T(8,128)(2,1)} %bitcast.31, s32[1024]{0:T(1024)S(1)} %pad_clamp_fusion), kind=kCustom, calls=%fused_computation.1 | custom fusion | bytes 1050624 | tf_op jit(solution)/shard_map/jit(_take)/gather | solution.py:68
  157.3 2.1 %multiply_reduce_fusion = bf16[64,512]{1,0:T(8,128)(2,1)} fusion(bf16[512,512]{1,0:T(8,128)(2,1)} %gather_fusion.1, f32[64,8]{1,0:T(8,128)S(1)} %copy.30, pred[64,8]{1,0:T(8,128)(4,1)S(1)} %compare_and_fusion), kind=kLoop, calls=%fused_computation.7 | loop fusion | flops 1015808 | bytes 592384 | tf_op jit(solution)/shard_map/reduce_sum | solution.py:71
  (22 shorter events, 0.6 us)
Async XLA Ops:
  6.5 110.1 %copy-start = (bf16[4,768,512]{2,1,0:T(8,128)(2,1)S(1)}, bf16[4,768,512]{2,1,0:T(8,128)(2,1)}, u32[]{:S(2)}) copy-start(bf16[4,768,512]{2,1,0:T(8,128)(2,1)} %param.9) | copy-start | bytes 9437188
  6.5 88.0 %reduce-scatter.2.cloned.1.call-start = ((), (), s32[]{:S(2)}) async-start(), calls=%async_computation.3 | async-start | bytes 3932160 | tf_op jit(solution)/shard_map/reduce_scatter | solution.py:19
  57.5 59.1 %all-gather.2.cloned.1.call-start = ((), (), s32[]{:S(2)}) async-start(), calls=%async_computation.4 | async-start | bytes 1966080 | tf_op jit(solution)/shard_map/all_gather | solution.py:30
  119.0 5.8 %copy-start.1 = (f32[64,8]{0,1:T(8,128)S(1)}, f32[64,8]{0,1:T(8,128)}, u32[]{:S(2)}) copy-start(f32[64,8]{0,1:T(8,128)} %param.7) | copy-start | bytes 6148
  120.1 30.8 %all-to-all-start.1 = ((bf16[4,4,64,512]{3,2,0,1:T(8,128)(2,1)}), bf16[4,4,64,512]{3,2,0,1:T(8,128)(2,1)}, u32[]{:S(2)}, u32[]{:S(2)}) async-start(bf16[4,4,64,512]{3,2,0,1:T(8,128)(2,1)} %copy.42), calls=%async_computation.2 | async-start | bytes 2097152 | tf_op jit(solution)/shard_map/all_to_all | solution.py:61
Sparse Core Ops, SparseCore 0:
  57.6 36.8 reduce-scatter.1
  96.9 19.6 all-gather.1
where the time goes:
time: 167 us; the launch traced here: 166 us
  waiting for transfers between devices  82.8 us (50%)
  blocking collectives  31.9 us (19%)
  local copies, waits for them, and re-layouts  17.6 us (11%)
  between operations  13.5 us (8%)
  matrix products  8.66 us (5%)
  other arithmetic  7.2 us (4%)
  starting transfers between devices  4.64 us (3%)
    reduce_scatter x1, waiting for transfers between devices, expert_block(): lax.psum_scatter(gate_up_terms(inputs, gate_up_w).astype(jnp.bfloat16), '...  37 us
    all_to_all x1, blocking collectives, per_device(): lax.all_to_all(outgoing, 'expert', split_axis=1, concat_axis=1, tiled=True)  31.9 us
    all_to_all x1, waiting for transfers between devices, per_device(): lax.all_to_all(expert_out.reshape(local_experts, n_expert, capacity, feat...  26 us
    all_gather x1, waiting for transfers between devices, expert_block(): lax.all_gather(hidden, 'token', axis=0, tiled=True)  19.8 us
    dot_general x1, matrix products, gate_up_terms(): jnp.einsum('erd,edf->ref', inputs, w_gate_up, preferred_element_type=jnp....  6.28 us
    gather x1, local copies, waits for them, and re-layouts, per_device(): jnp.take(padded, slot_table, axis=0)  5.06 us
    all_to_all x1, starting transfers between devices, per_device(): lax.all_to_all(expert_out.reshape(local_experts, n_expert, capacity, feat...  4.6 us
    gather x1, local copies, waits for them, and re-layouts, per_device(): jnp.take(returned.reshape(local_experts * slot_count, feature_cols), posi...  4.01 us
  transfers between devices with their start and end apart: 3, of which 3 were waited for; matrix products, arithmetic and copies ran while one was open for 0% of the time, Pallas kernels for 0%

commit v1 on v0

--- a/solution.py
+++ b/solution.py
@@ -1,7 +1,13 @@
+import functools
+
 import jax
 import jax.numpy as jnp
 from jax import lax
+from jax.experimental import pallas as pl
+from jax.experimental.pallas import tpu as pltpu
 from jax.sharding import PartitionSpec as P
+
+MESH = pl.DeviceIdType.MESH
 
 
 def rank_slots(flat_ids, experts):
@@ -34,7 +40,7 @@
     return produced.astype(jnp.bfloat16)
 
 
-def per_device(tokens, expert_ids, route_weights, w_gate_up, w_down):
+def slot_device(tokens, expert_ids, route_weights, w_gate_up, w_down):
     tok_dev, feature_cols = tokens.shape
     top_k = expert_ids.shape[1]
     local_experts = w_gate_up.shape[0]
@@ -70,6 +76,257 @@
     ).reshape(tok_dev, top_k, feature_cols)
     combined = jnp.sum(route_weights[:, :, None] * picked.astype(jnp.float32), axis=1)
     return combined.astype(jnp.bfloat16)
+
+
+def flip(index, bits):
+    out, bit = index, 1
+    while bit <= bits:
+        if bits & bit:
+            out = out + bit * (1 - 2 * ((index // bit) % 2))
+        bit *= 2
+    return out
+
+
+def dense_kernel(
+    order,
+    tokens_ref,
+    ids_ref,
+    weights_ref,
+    wg_hbm,
+    wd_hbm,
+    out_ref,
+    wg,
+    wd,
+    tok,
+    row_out,
+    row_in,
+    far_out,
+    far_in,
+    sum_out,
+    sum_in,
+    near_out,
+    near_in,
+    own,
+    hid,
+    back_out,
+    back_in,
+    total,
+    wg_sem,
+    wd_sem,
+    tok_s,
+    tok_r,
+    row_s,
+    row_r,
+    far_s,
+    far_r,
+    sum_s,
+    sum_r,
+    near_s,
+    near_r,
+    hid_s,
+    hid_r,
+    back_s,
+    back_r,
+):
+    z = lax.axis_index("expert")
+    t = lax.axis_index("token")
+    n_e = len(order)
+    rows = tokens_ref.shape[0]
+    half = own.shape[2] // 2
+    local = wg.shape[0]
+    f32, bf16 = jnp.float32, jnp.bfloat16
+    mate, across = {"token": flip(t, 1)}, {"token": flip(t, 2)}
+
+    barrier = pltpu.get_barrier_semaphore()
+    partners = [{"expert": flip(z, k)} for k in order if k] + [mate, across]
+    for partner in partners:
+        pl.semaphore_signal(barrier, inc=1, device_id=partner, device_id_type=MESH)
+
+    wg_copies, wd_copies = {}, {}
+    for j in (3, 1, 2, 0):
+        wg_copies[j] = pltpu.make_async_copy(wg_hbm.at[flip(t, j)], wg.at[j], wg_sem.at[j])
+        wg_copies[j].start()
+    for j in range(local):
+        wd_copies[j] = pltpu.make_async_copy(wd_hbm.at[flip(t, j)], wd.at[j], wd_sem.at[j])
+        wd_copies[j].start()
+
+    lanes = row_out.shape[2]
+    eye = lax.broadcasted_iota(jnp.int32, (rows, lanes), 0) == lax.broadcasted_iota(
+        jnp.int32, (rows, lanes), 1
+    )
+    for k in order:
+        expert = flip(z, k) * local + t
+        column = jnp.sum(
+            jnp.where(ids_ref[...] == expert, weights_ref[...], 0.0), axis=1, keepdims=True
+        )
+        row = jnp.sum(jnp.where(eye, column, 0.0), axis=0, keepdims=True)
+        row_out[k] = jnp.broadcast_to(row, row_out.shape[1:])
+
+    pl.semaphore_wait(barrier, len(partners))
+
+    pending = []
+
+    def send(src, dst, s_sem, r_sem, device):
+        copy = pltpu.make_async_remote_copy(
+            src_ref=src,
+            dst_ref=dst,
+            send_sem=s_sem,
+            recv_sem=r_sem,
+            device_id=device,
+            device_id_type=MESH,
+        )
+        copy.start()
+        pending.append(copy)
+        return copy
+
+    tok_c, row_c, far_c, sum_c, near_c, back_c = {}, {}, {}, {}, {}, {}
+    hid_c = {}
+    for k in order:
+        if k:
+            tok_c[k] = send(
+                tokens_ref, tok.at[k], tok_s.at[k], tok_r.at[k], {"expert": flip(z, k)}
+            )
+    for k in order:
+        if k:
+            row_c[k] = send(
+                row_out.at[k], row_in.at[k], row_s.at[k], row_r.at[k], {"expert": flip(z, k)}
+            )
+
+    def terms(k, j):
+        x = tok[k] if k else tokens_ref[...]
+        return jnp.dot(x, wg[j], preferred_element_type=f32)
+
+    def stage_a(k):
+        first = k == order[0]
+        if k:
+            tok_c[k].wait_recv()
+        if first:
+            wg_copies[3].wait()
+        far_out[k] = terms(k, 3).astype(bf16)
+        far_c[k] = send(far_out.at[k], far_in.at[k], far_s.at[k], far_r.at[k], mate)
+        if first:
+            wg_copies[1].wait()
+        near_out[k] = terms(k, 1).astype(bf16)
+        near_c[k] = send(near_out.at[k], near_in.at[k], near_s.at[k], near_r.at[k], mate)
+        if first:
+            wg_copies[2].wait()
+        own[k] = terms(k, 2)
+        far_c[k].wait_recv()
+        sum_out[k] = (own[k] + far_in[k].astype(f32)).astype(bf16)
+        sum_c[k] = send(sum_out.at[k], sum_in.at[k], sum_s.at[k], sum_r.at[k], across)
+        if first:
+            wg_copies[0].wait()
+        own[k] = terms(k, 0)
+
+    def stage_b(k):
+        near_c[k].wait_recv()
+        if k:
+            row_c[k].wait_recv()
+        row = row_in[k, :1, :] if k else row_out[k, :1, :]
+        column = jnp.sum(jnp.where(eye, row, 0.0), axis=1, keepdims=True)
+        sum_c[k].wait_recv()
+        gate = own[k, :, :half] + near_in[k, :, :half].astype(f32) + sum_in[k, :, :half].astype(f32)
+        up = own[k, :, half:] + near_in[k, :, half:].astype(f32) + sum_in[k, :, half:].astype(f32)
+        hid[k, 0] = (gate / (1.0 + jnp.exp(-gate)) * up * column).astype(bf16)
+        hid_c[k, 2] = send(hid.at[k, 0], hid.at[k, 2], hid_s.at[k, 2], hid_r.at[k, 2], across)
+        hid_c[k, 1] = send(hid.at[k, 0], hid.at[k, 1], hid_s.at[k, 1], hid_r.at[k, 1], mate)
+
+    def stage_f(k):
+        hid_c[k, 2].wait_recv()
+        hid_c[k, 3] = send(hid.at[k, 2], hid.at[k, 3], hid_s.at[k, 3], hid_r.at[k, 3], mate)
+
+    def stage_c(k):
+        if k == order[0]:
+            for j in range(local):
+                wd_copies[j].wait()
+        acc = jnp.dot(hid[k, 0], wd[0], preferred_element_type=f32)
+        hid_c[k, 1].wait_recv()
+        acc = acc + jnp.dot(hid[k, 1], wd[1], preferred_element_type=f32)
+        acc = acc + jnp.dot(hid[k, 2], wd[2], preferred_element_type=f32)
+        hid_c[k, 3].wait_recv()
+        acc = acc + jnp.dot(hid[k, 3], wd[3], preferred_element_type=f32)
+        if k:
+            back_out[k] = acc.astype(bf16)
+            back_c[k] = send(
+                back_out.at[k], back_in.at[k], back_s.at[k], back_r.at[k], {"expert": flip(z, k)}
+            )
+        else:
+            total[...] = acc
+
+    n = n_e
+    for step in range(n + 3):
+        if step < n:
+            stage_a(order[step])
+        if 0 <= step - 2 < n:
+            stage_f(order[step - 2])
+        if 0 <= step - 1 < n:
+            stage_b(order[step - 1])
+        if 0 <= step - 2 < n:
+            stage_c(order[step - 2])
+
+    result = total[...]
+    for k in order:
+        if k:
+            back_c[k].wait_recv()
+            result = result + back_in[k].astype(f32)
+    out_ref[...] = result.astype(out_ref.dtype)
+    for copy in pending:
+        copy.wait_send()
+
+
+def dense_device(tokens, expert_ids, route_weights, w_gate_up, w_down):
+    rows, feature_cols = tokens.shape
+    local, _, wide = w_gate_up.shape
+    hidden_units, out_cols = w_down.shape[1:]
+    n_e = lax.axis_size("expert")
+    order = tuple(sorted(range(n_e), key=lambda k: (k != 0, k == 1, k)))
+    f32, bf16 = jnp.float32, jnp.bfloat16
+    vmem = pl.BlockSpec(memory_space=pltpu.VMEM)
+    hbm = pl.BlockSpec(memory_space=pl.ANY)
+    dma = pltpu.SemaphoreType.DMA
+    lanes = -(-rows // 128) * 128
+    return pl.pallas_call(
+        functools.partial(dense_kernel, order),
+        out_shape=jax.ShapeDtypeStruct((rows, out_cols), bf16),
+        in_specs=[vmem, vmem, vmem, hbm, hbm],
+        out_specs=vmem,
+        scratch_shapes=[
+            pltpu.VMEM(w_gate_up.shape, bf16),
+            pltpu.VMEM(w_down.shape, bf16),
+            pltpu.VMEM((n_e, rows, feature_cols), bf16),
+            pltpu.VMEM((n_e, 8, lanes), f32),
+            pltpu.VMEM((n_e, 8, lanes), f32),
+            *[pltpu.VMEM((n_e, rows, wide), bf16)] * 6,
+            pltpu.VMEM((n_e, rows, wide), f32),
+            pltpu.VMEM((n_e, local, rows, hidden_units), bf16),
+            pltpu.VMEM((n_e, rows, out_cols), bf16),
+            pltpu.VMEM((n_e, rows, out_cols), bf16),
+            pltpu.VMEM((rows, out_cols), f32),
+            dma((local,)),
+            dma((local,)),
+            *[dma((n_e,))] * 10,
+            dma((n_e, local)),
+            dma((n_e, local)),
+            dma((n_e,)),
+            dma((n_e,)),
+        ],
+        compiler_params=pltpu.CompilerParams(
+            collective_id=0, has_side_effects=True, vmem_limit_bytes=48 * 1024 * 1024
+        ),
+    )(tokens, expert_ids, route_weights, w_gate_up, w_down)
+
+
+def per_device(tokens, expert_ids, route_weights, w_gate_up, w_down):
+    tok_dev = tokens.shape[0]
+    top_k = expert_ids.shape[1]
+    local_experts = w_gate_up.shape[0]
+    n_expert, n_token = lax.axis_size("expert"), lax.axis_size("token")
+    experts = local_experts * n_expert
+    capacity = max(2, min(tok_dev, tok_dev * top_k * 5 // (2 * experts)))
+    dense = capacity >= tok_dev and n_expert & (n_expert - 1) == 0
+    if dense and n_token == local_experts == 4:
+        return dense_device(tokens, expert_ids, route_weights, w_gate_up, w_down)
+    return slot_device(tokens, expert_ids, route_weights, w_gate_up, w_down)
 
 
 def solution(mesh):

time: 167 us -> 47.9 us (0.29)
  waiting for transfers between devices: 82.8 us -> 0 us
  Pallas kernels: 0 us -> 42.7 us
  blocking collectives: 31.9 us -> 0 us
  between operations: 13.5 us -> 0.01 us
  local copies, waits for them, and re-layouts: 17.6 us -> 4.9 us
  matrix products: 8.66 us -> 0 us
  other arithmetic: 7.2 us -> 0 us
  starting transfers between devices: 4.64 us -> 0 us
    pallas_call x0 -> x1, Pallas kernels: none -> 42.7 us  [dense_device(): pl.pallas_call(functools.partial(dense_kernel, order), out_shape=jax.Shap...]
    reduce_scatter x1 -> x0, waiting for transfers between devices: 37 us -> none  [expert_block(): lax.psum_scatter(gate_up_terms(inputs, gate_up_w).astype(jnp.bfloat16), '...]
    all_to_all x1 -> x0, blocking collectives: 31.9 us -> none  [per_device(): lax.all_to_all(outgoing, 'expert', split_axis=1, concat_axis=1, tiled=True)]
    all_to_all x1 -> x0, waiting for transfers between devices: 26 us -> none  [per_device(): lax.all_to_all(expert_out.reshape(local_experts, n_expert, capacity, feat...]
    all_gather x1 -> x0, waiting for transfers between devices: 19.8 us -> none  [expert_block(): lax.all_gather(hidden, 'token', axis=0, tiled=True)]
    gather x2 -> x0, local copies, waits for them, and re-layouts: 9.07 us -> none  [the longest x1 5.06 us: per_device(): jnp.take(padded, slot_table, axis=0)]
    dot_general x2 -> x0, matrix products: 8.66 us -> none  [the longest x1 6.28 us: gate_up_terms(): jnp.einsum('erd,edf->ref', inputs, w_gate_up, preferred_element_type=jnp....]
    all_to_all x1 -> x0, starting transfers between devices: 4.6 us -> none  [per_device(): lax.all_to_all(expert_out.reshape(local_experts, n_expert, capacity, feat...]
  transfers between devices with their start and end apart: 3 -> 0, of which waited for: 3 -> 0; matrix products, arithmetic and copies ran while one was open for 0% -> 0% of each run, Pallas kernels for 0% -> 0%
where the time goes in v1:
time: 47.9 us; the launch traced here: 47.6 us
  Pallas kernels  42.7 us (89%)
  local copies, waits for them, and re-layouts  4.9 us (10%)
    pallas_call x1, Pallas kernels, dense_device(): pl.pallas_call(functools.partial(dense_kernel, order), out_shape=jax.Shap...  42.7 us
    unnamed x7, local copies, waits for them, and re-layouts  4.9 us

profile of v1, /device:TPU:0, one launch (start us, length us, event | category | flops | bytes accessed | tf_op | source)
XLA Modules:
  0.0 47.6 jit_solution(17754334144307653365)
XLA Ops:
  0.0 0.8 %copy.6.ids_ref = s32[64,8]{1,0:T(8,128)S(1)} copy(s32[64,8]{0,1:T(8,128)} %param.6) | data formatting | bytes 4096 | tf_op args[1]
  0.8 0.8 %copy.7.weights_ref = f32[64,8]{1,0:T(8,128)S(1)} copy(f32[64,8]{0,1:T(8,128)} %param.7) | data formatting | bytes 4096 | tf_op args[2]
  1.5 0.0 copy-start
  1.5 1.9 %copy-done = bf16[4,768,512]{2,1,0:T(8,128)(2,1)S(1)} copy-done((bf16[4,768,512]{2,1,0:T(8,128)(2,1)S(1)}, bf16[4,768,512]{2,1,0:T(8,128)(2,1)}, u32[]{:S(2)}) %copy-start) | copy-done | bytes 3145752
  3.4 0.0 copy-start.1
  3.4 0.8 %copy-done.1 = bf16[64,512]{1,0:T(8,128)(2,1)S(1)} copy-done((bf16[64,512]{1,0:T(8,128)(2,1)S(1)}, bf16[64,512]{1,0:T(8,128)(2,1)}, u32[]{:S(2)}) %copy-start.1) | copy-done | bytes 65560
  4.3 42.7 %shard_map.55 = bf16[64,512]{1,0:T(8,128)(2,1)S(1)} custom-call(bf16[64,512]{1,0:T(8,128)(2,1)S(1)} %copy-done.1, s32[64,8]{1,0:T(8,128)S(1)} %copy.6.ids_ref, f32[64,8]{1,0:T(8,128)S(1)} %copy.7.weights_ref, bf16[4,512,1536]{2,1,0:T(8,128)(2,1)} %wg_hbm.1, bf16[4,768,512]{2,1,0:T(8,128)(2,1)S(1)} %copy-done), custom_call_target="tpu_custom_call" | custom-call | tf_op jit(solution)/shard_map/pallas_call | solution.py:288
  47.0 0.6 %copy.9 = bf16[64,512]{1,0:T(8,128)(2,1)} copy(bf16[64,512]{1,0:T(8,128)(2,1)S(1)} %shard_map.55) | data formatting | bytes 131072
Async XLA Ops:
  1.5 1.9 %copy-start = (bf16[4,768,512]{2,1,0:T(8,128)(2,1)S(1)}, bf16[4,768,512]{2,1,0:T(8,128)(2,1)}, u32[]{:S(2)}) copy-start(bf16[4,768,512]{2,1,0:T(8,128)(2,1)} %wd_hbm.1) | copy-start | bytes 9437188
  3.4 0.8 %copy-start.1 = (bf16[64,512]{1,0:T(8,128)(2,1)S(1)}, bf16[64,512]{1,0:T(8,128)(2,1)}, u32[]{:S(2)}) copy-start(bf16[64,512]{1,0:T(8,128)(2,1)} %tokens_ref.1) | copy-start | bytes 196612

commit v2 on v1

v2 whole, which is shorter than its diff:
```python
import functools

import jax
import jax.numpy as jnp
from jax import lax
from jax.experimental import pallas as pl
from jax.experimental.pallas import tpu as pltpu
from jax.sharding import PartitionSpec as P

MESH = pl.DeviceIdType.MESH


def rank_slots(flat_ids, experts):
    onehot = (flat_ids[:, None] == jnp.arange(experts, dtype=jnp.int32)[None, :]).astype(jnp.int32)
    rank_of = jnp.sum((jnp.cumsum(onehot, axis=0) - 1) * onehot, axis=1)
    return (onehot, rank_of)


def gate_up_terms(inputs, w_gate_up):
    return jnp.einsum("erd,edf->ref", inputs, w_gate_up, preferred_element_type=jnp.float32)


def expert_block(inputs, gate_up_w, down_w):
    hidden_units = gate_up_w.shape[2] // 2
    summed = lax.psum_scatter(
        gate_up_terms(inputs, gate_up_w).astype(jnp.bfloat16),
        "token",
        scatter_dimension=0,
        tiled=True,
    ).astype(jnp.float32)
    hidden = (jax.nn.silu(summed[..., :hidden_units]) * summed[..., hidden_units:]).astype(
        jnp.bfloat16
    )
    produced = jnp.einsum(
        "reh,ehd->erd",
        lax.all_gather(hidden, "token", axis=0, tiled=True),
        down_w,
        preferred_element_type=jnp.float32,
    )
    return produced.astype(jnp.bfloat16)


def slot_device(tokens, expert_ids, route_weights, w_gate_up, w_down):
    tok_dev, feature_cols = tokens.shape
    top_k = expert_ids.shape[1]
    local_experts = w_gate_up.shape[0]
    n_expert = lax.axis_size("expert")
    experts = local_experts * n_expert
    capacity = max(2, min(tok_dev, tok_dev * top_k * 5 // (2 * experts)))
    slot_count = n_expert * capacity
    flat_ids = expert_ids.reshape(-1)
    onehot, rank_of = rank_slots(flat_ids, experts)
    position = (
        flat_ids % local_experts * slot_count + flat_ids // local_experts * capacity + rank_of
    )
    token_of = jnp.arange(flat_ids.shape[0], dtype=jnp.int32) // top_k
    slot_table = (
        jnp.full((local_experts * slot_count,), tok_dev, jnp.int32).at[position].set(token_of)
    )
    padded = jnp.concatenate([tokens, jnp.zeros((1, feature_cols), tokens.dtype)], axis=0)
    outgoing = jnp.take(padded, slot_table, axis=0).reshape(
        local_experts, n_expert, capacity, feature_cols
    )
    arrived = lax.all_to_all(outgoing, "expert", split_axis=1, concat_axis=1, tiled=True)
    inputs = arrived.reshape(local_experts, slot_count, feature_cols)
    expert_out = expert_block(inputs, w_gate_up, w_down)
    returned = lax.all_to_all(
        expert_out.reshape(local_experts, n_expert, capacity, feature_cols),
        "expert",
        split_axis=1,
        concat_axis=1,
        tiled=True,
    )
    picked = jnp.take(
        returned.reshape(local_experts * slot_count, feature_cols), position, axis=0
    ).reshape(tok_dev, top_k, feature_cols)
    combined = jnp.sum(route_weights[:, :, None] * picked.astype(jnp.float32), axis=1)
    return combined.astype(jnp.bfloat16)


def flip(index, bits):
    out, bit = index, 1
    while bit <= bits:
        if bits & bit:
            out = out + bit * (1 - 2 * ((index // bit) % 2))
        bit *= 2
    return out


def dense_kernel(
    chunks,
    tokens_ref,
    ids_ref,
    weights_ref,
    wg_hbm,
    wd_hbm,
    out_ref,
    wg,
    wd,
    tok,
    row_out,
    row_in,
    far_out,
    far_in,
    sum_out,
    sum_in,
    near_out,
    near_in,
    part,
    own,
    hid,
    back_out,
    back_in,
    total,
    load_sem,
    wg_sem,
    wd_sem,
    tok_s,
    tok_r,
    row_s,
    row_r,
    far_s,
    far_r,
    sum_s,
    sum_r,
    near_s,
    near_r,
    hid_s,
    hid_r,
    back_s,
    back_r,
):
    z = lax.axis_index("expert")
    t = lax.axis_index("token")
    rows = tokens_ref.shape[0]
    half = own.shape[2] // 2
    local = wg.shape[0]
    f32, bf16 = jnp.float32, jnp.bfloat16
    mate, across = {"token": flip(t, 1)}, {"token": flip(t, 2)}
    others = []
    for k, _, _ in chunks:
        if k and k not in others:
            others.append(k)
    others.sort()

    barrier = pltpu.get_barrier_semaphore()
    partners = [mate, across] + [{"expert": flip(z, k)} for k in others]
    for partner in reversed(partners):
        pl.semaphore_signal(barrier, inc=1, device_id=partner, device_id_type=MESH)

    load = pltpu.make_async_copy(tokens_ref, tok.at[0], load_sem)
    load.start()
    wg_copies, wd_copies = {}, {}
    for j in (3, 2, 1, 0):
        wg_copies[j] = pltpu.make_async_copy(wg_hbm.at[flip(t, j)], wg.at[j], wg_sem.at[j])
        wg_copies[j].start()

    for k in [0] + others:
        expert = flip(z, k) * local + t
        row = jnp.sum(
            jnp.where(ids_ref[...] == expert, weights_ref[...], 0.0), axis=0, keepdims=True
        )
        row_out[k] = jnp.broadcast_to(row, row_out.shape[1:])

    pending = []

    def send(src, dst, s_sem, r_sem, device):
        copy = pltpu.make_async_remote_copy(
            src_ref=src,
            dst_ref=dst,
            send_sem=s_sem,
            recv_sem=r_sem,
            device_id=device,
            device_id_type=MESH,
        )
        copy.start()
        pending.append(copy)
        return copy

    tok_c, row_c, far_c, sum_c, near_c, back_c = {}, {}, {}, {}, {}, {}
    hid_c = {}

    def terms(c, j):
        k, start, size = chunks[c]
        return jnp.dot(tok[k, pl.ds(start, size), :], wg[j], preferred_element_type=f32)

    def piece(c):
        k, start, size = chunks[c]
        return (k, pl.ds(start, size))

    def stage_a(c):
        k = chunks[c][0]
        here = piece(c)
        if k:
            tok_c[k].wait_recv()
        if c == 0:
            load.wait()
            wg_copies[3].wait()
        far_out[here] = terms(c, 3).astype(bf16)
        if c == 0:
            pl.semaphore_wait(barrier, len(partners))
        far_c[c] = send(far_out.at[here], far_in.at[here], far_s.at[c], far_r.at[c], mate)
        if c == 0:
            for o in others:
                there = {"expert": flip(z, o)}
                tok_c[o] = send(tokens_ref, tok.at[o], tok_s.at[o], tok_r.at[o], there)
            for j in range(local):
                wd_copies[j] = pltpu.make_async_copy(
                    wd_hbm.at[flip(t, j)], wd.at[j], wd_sem.at[j]
                )
                wd_copies[j].start()
            wg_copies[2].wait()
        part[here] = terms(c, 2)
        if c == 0:
            far_c[c].wait_recv()
            sum_out[here] = (part[here] + far_in[here].astype(f32)).astype(bf16)
            sum_c[c] = send(sum_out.at[here], sum_in.at[here], sum_s.at[c], sum_r.at[c], across)
            for o in others:
                there = {"expert": flip(z, o)}
                row_c[o] = send(row_out.at[o], row_in.at[o], row_s.at[o], row_r.at[o], there)
            wg_copies[1].wait()
        near_out[here] = terms(c, 1).astype(bf16)
        near_c[c] = send(near_out.at[here], near_in.at[here], near_s.at[c], near_r.at[c], mate)
        if c == 0:
            wg_copies[0].wait()
            own[here] = terms(c, 0)
            return
        far_c[c].wait_recv()
        sum_out[here] = (part[here] + far_in[here].astype(f32)).astype(bf16)
        sum_c[c] = send(sum_out.at[here], sum_in.at[here], sum_s.at[c], sum_r.at[c], across)
        own[here] = terms(c, 0)

    def stage_b(c):
        k, start, size = chunks[c]
        here = piece(c)
        near_c[c].wait_recv()
        if k:
            row_c[k].wait_recv()
        row = row_in[k, :1, :] if k else row_out[k, :1, :]
        eye = start + lax.broadcasted_iota(
            jnp.int32, (size, rows), 0
        ) == lax.broadcasted_iota(jnp.int32, (size, rows), 1)
        column = jnp.sum(jnp.where(eye, row, 0.0), axis=1, keepdims=True)
        sum_c[c].wait_recv()
        gate_up = own[here] + near_in[here].astype(f32) + sum_in[here].astype(f32)
        gate, up = gate_up[:, :half], gate_up[:, half:]
        at = pl.ds(start, size)
        hid[k, 0, at] = (gate / (1.0 + jnp.exp(-gate)) * up * column).astype(bf16)
        for j, device in ((2, across), (1, mate)):
            hid_c[c, j] = send(
                hid.at[k, 0, at], hid.at[k, j, at], hid_s.at[c, j], hid_r.at[c, j], device
            )

    def stage_f(c):
        k, start, size = chunks[c]
        at = pl.ds(start, size)
        hid_c[c, 2].wait_recv()
        hid_c[c, 3] = send(
            hid.at[k, 2, at], hid.at[k, 3, at], hid_s.at[c, 3], hid_r.at[c, 3], mate
        )

    def stage_c(c):
        k, start, size = chunks[c]
        at = pl.ds(start, size)
        if c == 0:
            for j in range(local):
                wd_copies[j].wait()
        acc = jnp.dot(hid[k, 0, at], wd[0], preferred_element_type=f32)
        hid_c[c, 1].wait_recv()
        acc = acc + jnp.dot(hid[k, 1, at], wd[1], preferred_element_type=f32)
        acc = acc + jnp.dot(hid[k, 2, at], wd[2], preferred_element_type=f32)
        hid_c[c, 3].wait_recv()
        acc = acc + jnp.dot(hid[k, 3, at], wd[3], preferred_element_type=f32)
        if k:
            back_out[k] = acc.astype(bf16)
            back_c[k] = send(
                back_out.at[k], back_in.at[k], back_s.at[k], back_r.at[k], {"expert": flip(z, k)}
            )
        else:
            total[at] = acc

    n = len(chunks)
    lead = 2
    for step in range(n + lead + 1):
        if step < n:
            stage_a(step)
        if 0 <= step - lead < n:
            stage_b(step - lead)
        if 0 <= step - lead - 1 < n:
            stage_f(step - lead - 1)
            stage_c(step - lead - 1)

    result = total[...]
    for k in others:
        back_c[k].wait_recv()
        result = result + back_in[k].astype(f32)
    out_ref[...] = result.astype(out_ref.dtype)
    for copy in pending:
        copy.wait_send()


def dense_device(tokens, expert_ids, route_weights, w_gate_up, w_down):
    rows, feature_cols = tokens.shape
    local, _, wide = w_gate_up.shape
    hidden_units, out_cols = w_down.shape[1:]
    n_e = lax.axis_size("expert")
    first = rows // 32 * 16
    chunks = ((0, 0, first),) + tuple((k, 0, rows) for k in (*range(2, n_e), 1))
    chunks += ((0, first, rows - first),)
    parts = len(chunks)
    f32, bf16 = jnp.float32, jnp.bfloat16
    vmem = pl.BlockSpec(memory_space=pltpu.VMEM)
    hbm = pl.BlockSpec(memory_space=pl.ANY)
    dma = pltpu.SemaphoreType.DMA
    return pl.pallas_call(
        functools.partial(dense_kernel, chunks),
        out_shape=jax.ShapeDtypeStruct((rows, out_cols), bf16),
        in_specs=[hbm, vmem, vmem, hbm, hbm],
        out_specs=vmem,
        scratch_shapes=[
            pltpu.VMEM(w_gate_up.shape, bf16),
            pltpu.VMEM(w_down.shape, bf16),
            pltpu.VMEM((n_e, rows, feature_cols), bf16),
            pltpu.VMEM((n_e, 8, rows), f32),
            pltpu.VMEM((n_e, 8, rows), f32),
            *[pltpu.VMEM((n_e, rows, wide), bf16)] * 6,
            *[pltpu.VMEM((n_e, rows, wide), f32)] * 2,
            pltpu.VMEM((n_e, local, rows, hidden_units), bf16),
            pltpu.VMEM((n_e, rows, out_cols), bf16),
            pltpu.VMEM((n_e, rows, out_cols), bf16),
            pltpu.VMEM((rows, out_cols), f32),
            dma,
            *[dma((local,))] * 2,
            *[dma((n_e,))] * 4,
            *[dma((parts,))] * 6,
            *[dma((parts, local))] * 2,
            dma((n_e,)),
            dma((n_e,)),
        ],
        compiler_params=pltpu.CompilerParams(
            collective_id=0, has_side_effects=True, vmem_limit_bytes=60 * 1024 * 1024
        ),
    )(tokens, expert_ids.T, route_weights.T, w_gate_up, w_down)


def per_device(tokens, expert_ids, route_weights, w_gate_up, w_down):
    tok_dev = tokens.shape[0]
    top_k = expert_ids.shape[1]
    local_experts = w_gate_up.shape[0]
    n_expert, n_token = lax.axis_size("expert"), lax.axis_size("token")
    experts = local_experts * n_expert
    capacity = max(2, min(tok_dev, tok_dev * top_k * 5 // (2 * experts)))
    dense = capacity >= tok_dev >= 32 and n_expert >= 2 and n_expert & (n_expert - 1) == 0
    if dense and tok_dev % 16 == 0 and n_token == local_experts == 4:
        return dense_device(tokens, expert_ids, route_weights, w_gate_up, w_down)
    return slot_device(tokens, expert_ids, route_weights, w_gate_up, w_down)


def solution(mesh):
    return jax.shard_map(
        per_device,
        mesh=mesh,
        in_specs=(
            P(("groups", "expert"), "token"),
            P(("groups", "expert"), None),
            P(("groups", "expert"), None),
            P("expert", "token", None),
            P("expert", None, "token"),
        ),
        out_specs=P(("groups", "expert"), "token"),
        check_vma=False,
    )
```

time: 47.9 us -> 47.5 us (level)
  local copies, waits for them, and re-layouts: 4.9 us -> 1.47 us
  Pallas kernels: 42.7 us -> 45.8 us
    unnamed x7 -> x1, local copies, waits for them, and re-layouts: 4.9 us -> 1.47 us
    pallas_call x1, Pallas kernels: 42.7 us -> 45.8 us  [dense_device(): pl.pallas_call(functools.partial(dense_kernel, chunks), out_shape=jax.Sha...]
where the time goes in v2:
time: 47.5 us; the launch traced here: 47.2 us
  Pallas kernels  45.8 us (96%)
  local copies, waits for them, and re-layouts  1.47 us (3%)
    pallas_call x1, Pallas kernels, dense_device(): pl.pallas_call(functools.partial(dense_kernel, chunks), out_shape=jax.Sha...  45.8 us
    unnamed x1, local copies, waits for them, and re-layouts  1.47 us

profile of v2, /device:TPU:0, one launch (start us, length us, event | category | flops | bytes accessed | tf_op | source)
XLA Modules:
  0.0 47.2 jit_solution(3843619245937642042)
XLA Ops:
  0.0 45.8 %shard_map.55 = bf16[64,512]{1,0:T(8,128)(2,1)} custom-call(bf16[64,512]{1,0:T(8,128)(2,1)} %tokens_ref.1, s32[8,64]{1,0:T(8,128)} %bitcast.2, f32[8,64]{1,0:T(8,128)} %bitcast.3, bf16[4,512,1536]{2,1,0:T(8,128)(2,1)} %wg_hbm.1, bf16[4,768,512]{2,1,0:T(8,128)(2,1)} %wd_hbm.1), custom_call_target="tpu_custom_call" | custom-call | tf_op jit(solution)/shard_map/pallas_call | solution.py:315
  45.8 1.5 %copy.7 = bf16[64,512]{1,0:T(8,128)(2,1)} copy(bf16[64,512]{1,0:T(8,128)(2,1)} %shard_map.55) | data formatting | bytes 131072

commit v3 on v2

--- a/solution.py
+++ b/solution.py
@@ -90,13 +90,15 @@
 def dense_kernel(
     chunks,
     tokens_ref,
-    ids_ref,
-    weights_ref,
+    ids_hbm,
+    weights_hbm,
     wg_hbm,
     wd_hbm,
     out_ref,
     wg,
     wd,
+    ids_ref,
+    weights_ref,
     tok,
     row_out,
     row_in,
@@ -141,19 +143,26 @@
     for k, _, _ in chunks:
         if k and k not in others:
             others.append(k)
-    others.sort()
 
     barrier = pltpu.get_barrier_semaphore()
     partners = [mate, across] + [{"expert": flip(z, k)} for k in others]
     for partner in reversed(partners):
         pl.semaphore_signal(barrier, inc=1, device_id=partner, device_id_type=MESH)
 
-    load = pltpu.make_async_copy(tokens_ref, tok.at[0], load_sem)
-    load.start()
+    loads = [
+        pltpu.make_async_copy(tokens_ref, tok.at[0], load_sem.at[0]),
+        pltpu.make_async_copy(ids_hbm, ids_ref, load_sem.at[1]),
+        pltpu.make_async_copy(weights_hbm, weights_ref, load_sem.at[2]),
+    ]
     wg_copies, wd_copies = {}, {}
     for j in (3, 2, 1, 0):
         wg_copies[j] = pltpu.make_async_copy(wg_hbm.at[flip(t, j)], wg.at[j], wg_sem.at[j])
+    for load in loads:
+        load.start()
+    for j in (3, 2):
         wg_copies[j].start()
+    for load in loads:
+        load.wait()
 
     for k in [0] + others:
         expert = flip(z, k) * local + t
@@ -191,19 +200,19 @@
     def stage_a(c):
         k = chunks[c][0]
         here = piece(c)
-        if k:
+        if k and chunks[c][1] == 0:
             tok_c[k].wait_recv()
         if c == 0:
-            load.wait()
-            wg_copies[3].wait()
-        far_out[here] = terms(c, 3).astype(bf16)
-        if c == 0:
             pl.semaphore_wait(barrier, len(partners))
-        far_c[c] = send(far_out.at[here], far_in.at[here], far_s.at[c], far_r.at[c], mate)
-        if c == 0:
             for o in others:
                 there = {"expert": flip(z, o)}
                 tok_c[o] = send(tokens_ref, tok.at[o], tok_s.at[o], tok_r.at[o], there)
+            for j in (1, 0):
+                wg_copies[j].start()
+            wg_copies[3].wait()
+        far_out[here] = terms(c, 3).astype(bf16)
+        far_c[c] = send(far_out.at[here], far_in.at[here], far_s.at[c], far_r.at[c], mate)
+        if c == 0:
             for j in range(local):
                 wd_copies[j] = pltpu.make_async_copy(
                     wd_hbm.at[flip(t, j)], wd.at[j], wd_sem.at[j]
@@ -234,7 +243,7 @@
         k, start, size = chunks[c]
         here = piece(c)
         near_c[c].wait_recv()
-        if k:
+        if k and start == 0:
             row_c[k].wait_recv()
         row = row_in[k, :1, :] if k else row_out[k, :1, :]
         eye = start + lax.broadcasted_iota(
@@ -272,27 +281,32 @@
         hid_c[c, 3].wait_recv()
         acc = acc + jnp.dot(hid[k, 3, at], wd[3], preferred_element_type=f32)
         if k:
-            back_out[k] = acc.astype(bf16)
-            back_c[k] = send(
-                back_out.at[k], back_in.at[k], back_s.at[k], back_r.at[k], {"expert": flip(z, k)}
+            there = {"expert": flip(z, k)}
+            back_out[k, at] = acc.astype(bf16)
+            back_c[c] = send(
+                back_out.at[k, at], back_in.at[k, at], back_s.at[c], back_r.at[c], there
             )
         else:
             total[at] = acc
 
     n = len(chunks)
-    lead = 2
-    for step in range(n + lead + 1):
-        if step < n:
-            stage_a(step)
-        if 0 <= step - lead < n:
-            stage_b(step - lead)
-        if 0 <= step - lead - 1 < n:
-            stage_f(step - lead - 1)
-            stage_c(step - lead - 1)
-
+    for step in range(n):
+        stage_a(step)
+        if step >= 2:
+            stage_b(step - 2)
+        if step >= 3:
+            stage_f(step - 3)
+            stage_c(step - 3)
+    for step in range(max(n - 2, 0), n):
+        stage_b(step)
+    for step in range(max(n - 3, 0), n):
+        stage_f(step)
+        stage_c(step)
+
+    for copy in back_c.values():
+        copy.wait_recv()
     result = total[...]
     for k in others:
-        back_c[k].wait_recv()
         result = result + back_in[k].astype(f32)
     out_ref[...] = result.astype(out_ref.dtype)
     for copy in pending:
@@ -305,21 +319,23 @@
     hidden_units, out_cols = w_down.shape[1:]
     n_e = lax.axis_size("expert")
     first = rows // 32 * 16
-    chunks = ((0, 0, first),) + tuple((k, 0, rows) for k in (*range(2, n_e), 1))
-    chunks += ((0, first, rows - first),)
+    chunks = ((0, 0, rows), (1, 0, first)) + tuple((k, 0, rows) for k in range(n_e - 1, 1, -1))
+    chunks += ((1, first, rows - first),)
     parts = len(chunks)
     f32, bf16 = jnp.float32, jnp.bfloat16
     vmem = pl.BlockSpec(memory_space=pltpu.VMEM)
-    hbm = pl.BlockSpec(memory_space=pl.ANY)
+    hbm = pl.BlockSpec(memory_space=pltpu.MemorySpace.HBM)
     dma = pltpu.SemaphoreType.DMA
     return pl.pallas_call(
         functools.partial(dense_kernel, chunks),
         out_shape=jax.ShapeDtypeStruct((rows, out_cols), bf16),
-        in_specs=[hbm, vmem, vmem, hbm, hbm],
+        in_specs=[hbm] * 5,
         out_specs=vmem,
         scratch_shapes=[
             pltpu.VMEM(w_gate_up.shape, bf16),
             pltpu.VMEM(w_down.shape, bf16),
+            pltpu.VMEM(expert_ids.shape[::-1], expert_ids.dtype),
+            pltpu.VMEM(route_weights.shape[::-1], f32),
             pltpu.VMEM((n_e, rows, feature_cols), bf16),
             pltpu.VMEM((n_e, 8, rows), f32),
             pltpu.VMEM((n_e, 8, rows), f32),
@@ -329,13 +345,12 @@
             pltpu.VMEM((n_e, rows, out_cols), bf16),
             pltpu.VMEM((n_e, rows, out_cols), bf16),
             pltpu.VMEM((rows, out_cols), f32),
-            dma,
+            dma((3,)),
             *[dma((local,))] * 2,
             *[dma((n_e,))] * 4,
             *[dma((parts,))] * 6,
             *[dma((parts, local))] * 2,
-            dma((n_e,)),
-            dma((n_e,)),
+            *[dma((parts,))] * 2,
         ],
         compiler_params=pltpu.CompilerParams(
             collective_id=0, has_side_effects=True, vmem_limit_bytes=60 * 1024 * 1024

time: 47.5 us -> 43.4 us (0.914)
  Pallas kernels: 45.8 us -> 41.7 us
    pallas_call x1, Pallas kernels: 45.8 us -> 41.7 us  [dense_device(): pl.pallas_call(functools.partial(dense_kernel, chunks), out_shape=jax.Sha...]
where the time goes in v3:
time: 43.4 us; the launch traced here: 43.2 us
  Pallas kernels  41.7 us (96%)
  local copies, waits for them, and re-layouts  1.47 us (3%)
    pallas_call x1, Pallas kernels, dense_device(): pl.pallas_call(functools.partial(dense_kernel, chunks), out_shape=jax.Sha...  41.7 us
    unnamed x1, local copies, waits for them, and re-layouts  1.47 us

profile of v3, /device:TPU:0, one launch (start us, length us, event | category | flops | bytes accessed | tf_op | source)
XLA Modules:
  0.0 43.2 jit_solution(7215695877283479121)
XLA Ops:
  0.0 41.7 %shard_map.55 = bf16[64,512]{1,0:T(8,128)(2,1)} custom-call(bf16[64,512]{1,0:T(8,128)(2,1)} %tokens_ref.1, s32[8,64]{1,0:T(8,128)} %bitcast.2, f32[8,64]{1,0:T(8,128)} %bitcast.3, bf16[4,512,1536]{2,1,0:T(8,128)(2,1)} %wg_hbm.1, bf16[4,768,512]{2,1,0:T(8,128)(2,1)} %wd_hbm.1), custom_call_target="tpu_custom_call" | custom-call | tf_op jit(solution)/shard_map/pallas_call | solution.py:329
  41.8 1.5 %copy.7 = bf16[64,512]{1,0:T(8,128)(2,1)} copy(bf16[64,512]{1,0:T(8,128)(2,1)} %shard_map.55) | data formatting | bytes 131072

commit v4 on v3

--- a/solution.py
+++ b/solution.py
@@ -203,14 +203,15 @@
         if k and chunks[c][1] == 0:
             tok_c[k].wait_recv()
         if c == 0:
+            wg_copies[3].wait()
+        far_out[here] = terms(c, 3).astype(bf16)
+        if c == 0:
             pl.semaphore_wait(barrier, len(partners))
             for o in others:
                 there = {"expert": flip(z, o)}
                 tok_c[o] = send(tokens_ref, tok.at[o], tok_s.at[o], tok_r.at[o], there)
             for j in (1, 0):
                 wg_copies[j].start()
-            wg_copies[3].wait()
-        far_out[here] = terms(c, 3).astype(bf16)
         far_c[c] = send(far_out.at[here], far_in.at[here], far_s.at[c], far_r.at[c], mate)
         if c == 0:
             for j in range(local):
@@ -290,18 +291,20 @@
             total[at] = acc
 
     n = len(chunks)
+    far, near = list(range(2, n - 1)), [1, n - 1]
     for step in range(n):
         stage_a(step)
-        if step >= 2:
-            stage_b(step - 2)
-        if step >= 3:
-            stage_f(step - 3)
-            stage_c(step - 3)
-    for step in range(max(n - 2, 0), n):
-        stage_b(step)
-    for step in range(max(n - 3, 0), n):
-        stage_f(step)
-        stage_c(step)
+        if step == 2:
+            stage_b(0)
+    for c in far[:1]:
+        stage_b(c)
+    stage_f(0)
+    stage_c(0)
+    for c in far[1:] + near:
+        stage_b(c)
+    for c in far + near:
+        stage_f(c)
+        stage_c(c)
 
     for copy in back_c.values():
         copy.wait_recv()

time: 43.4 us -> 43.7 us (level)
  no operation moved by 1% of the time
where the time goes in v4:
time: 43.7 us; the launch traced here: 43.6 us
  Pallas kernels  42.1 us (96%)
  local copies, waits for them, and re-layouts  1.47 us (3%)
    pallas_call x1, Pallas kernels, dense_device(): pl.pallas_call(functools.partial(dense_kernel, chunks), out_shape=jax.Sha...  42.1 us
    unnamed x1, local copies, waits for them, and re-layouts  1.47 us

profile of v4, /device:TPU:0, one launch (start us, length us, event | category | flops | bytes accessed | tf_op | source)
XLA Modules:
  0.0 43.6 jit_solution(16095511656185787243)
XLA Ops:
  0.0 42.1 %shard_map.55 = bf16[64,512]{1,0:T(8,128)(2,1)} custom-call(bf16[64,512]{1,0:T(8,128)(2,1)} %tokens_ref.1, s32[8,64]{1,0:T(8,128)} %bitcast.2, f32[8,64]{1,0:T(8,128)} %bitcast.3, bf16[4,512,1536]{2,1,0:T(8,128)(2,1)} %wg_hbm.1, bf16[4,768,512]{2,1,0:T(8,128)(2,1)} %wd_hbm.1), custom_call_target="tpu_custom_call" | custom-call | tf_op jit(solution)/shard_map/pallas_call | solution.py:332
  42.1 1.5 %copy.7 = bf16[64,512]{1,0:T(8,128)(2,1)} copy(bf16[64,512]{1,0:T(8,128)(2,1)} %shard_map.55) | data formatting | bytes 131072

commit v5 on v4

--- a/solution.py
+++ b/solution.py
@@ -203,15 +203,14 @@
         if k and chunks[c][1] == 0:
             tok_c[k].wait_recv()
         if c == 0:
-            wg_copies[3].wait()
-        far_out[here] = terms(c, 3).astype(bf16)
-        if c == 0:
             pl.semaphore_wait(barrier, len(partners))
             for o in others:
                 there = {"expert": flip(z, o)}
                 tok_c[o] = send(tokens_ref, tok.at[o], tok_s.at[o], tok_r.at[o], there)
             for j in (1, 0):
                 wg_copies[j].start()
+            wg_copies[3].wait()
+        far_out[here] = terms(c, 3).astype(bf16)
         far_c[c] = send(far_out.at[here], far_in.at[here], far_s.at[c], far_r.at[c], mate)
         if c == 0:
             for j in range(local):

time: 43.7 us -> 43.2 us (0.989)
  Pallas kernels: 42.1 us -> 41.5 us
    pallas_call x1, Pallas kernels: 42.1 us -> 41.5 us  [dense_device(): pl.pallas_call(functools.partial(dense_kernel, chunks), out_shape=jax.Sha...]
where the time goes in v5:
time: 43.2 us; the launch traced here: 43 us
  Pallas kernels  41.5 us (96%)
  local copies, waits for them, and re-layouts  1.47 us (3%)
    pallas_call x1, Pallas kernels, dense_device(): pl.pallas_call(functools.partial(dense_kernel, chunks), out_shape=jax.Sha...  41.5 us
    unnamed x1, local copies, waits for them, and re-layouts  1.47 us

profile of v5, /device:TPU:0, one launch (start us, length us, event | category | flops | bytes accessed | tf_op | source)
XLA Modules:
  0.0 43.0 jit_solution(5390536954985177457)
XLA Ops:
  0.0 41.5 %shard_map.55 = bf16[64,512]{1,0:T(8,128)(2,1)} custom-call(bf16[64,512]{1,0:T(8,128)(2,1)} %tokens_ref.1, s32[8,64]{1,0:T(8,128)} %bitcast.2, f32[8,64]{1,0:T(8,128)} %bitcast.3, bf16[4,512,1536]{2,1,0:T(8,128)(2,1)} %wg_hbm.1, bf16[4,768,512]{2,1,0:T(8,128)(2,1)} %wd_hbm.1), custom_call_target="tpu_custom_call" | custom-call | tf_op jit(solution)/shard_map/pallas_call | solution.py:331
  41.5 1.5 %copy.7 = bf16[64,512]{1,0:T(8,128)(2,1)} copy(bf16[64,512]{1,0:T(8,128)(2,1)} %shard_map.55) | data formatting | bytes 131072
